TPU v7x, 512 devices: a whole 4x4x16 slice. The times are simulated.
512 devices in a mesh: ctx: 64 (over z, x), ch: 8 (over y, core).
Axes of the slice: x: 4, y: 4, z: 16, core: 2. Of those that a mesh axis runs over, the one named last changes fastest.
Arguments:
- gate_input: bfloat16 [16384, 4096], P('ctx', 'ch'), may hold values from -6 to 6
- key_input: bfloat16 [16384, 4096], P('ctx', 'ch'), may hold values from -6 to 6
- value_input: bfloat16 [16384, 4096], P('ctx', 'ch'), may hold values from -6 to 6
- decay_rate: float32 [16, 4096], P(None, 'ch'), may hold values from 0.00012207031 to 0.26666667
- frequency: float32 [16, 4096], P(None, 'ch'), may hold values from 0 to 2.4
- residue: float32 [2, 16, 4096], P(None, None, 'ch'), may hold values from -2 to 2
- skip_gain: float32 [4096], P('ch'), may hold values from -3 to 3
- out_weight: bfloat16 [4096, 4096], P('ctx', 'ch'), may hold values from -0.09375 to 0.09375
Outputs:
- mixed: bfloat16 [16384, 4096], P('ctx', 'ch')
All inputs are finite; a program needn't handle non-finite values.
Results may differ from a plain program's by a relative error of at most 0.014.
Values may be sent and summed in bfloat16 or wider, within the bound.
A program may use at most 128 MiB of HBM per device.

v0:
```python
import jax
import jax.numpy as jnp
from jax import lax
from jax.sharding import PartitionSpec as P


def entering(value, axis, join, neutral):
    count, mine = (lax.axis_size(axis), lax.axis_index(axis))
    pieces = jax.tree.map(lambda part: lax.all_gather(part, axis), value)
    so_far = jax.tree.map(
        lambda part, zero: jnp.full_like(part, 0) + jnp.asarray(zero, part.dtype), value, neutral
    )

    def hop(position, so_far):
        longer = join(so_far, jax.tree.map(lambda part: part[position], pieces))
        return jax.tree.map(lambda new, old: jnp.where(position < mine, new, old), longer, so_far)

    return lax.fori_loop(0, count - 1, hop, so_far)


def cmul(a_re, a_im, b_re, b_im):
    return (a_re * b_re - a_im * b_im, a_re * b_im + a_im * b_re)


def filter_tables(decay_rate, frequency, residue, block_len):
    damping = 0.125 * decay_rate
    turning = 0.125 * frequency
    scaling = jnp.sqrt(2.0 * damping)
    coef_re = scaling * residue[0]
    coef_im = scaling * residue[1]
    offsets = jnp.arange(block_len).astype(jnp.float32)

    def powers(counts):
        fading = jnp.exp(-damping[None] * counts[:, None, None])
        phase = turning[None] * counts[:, None, None]
        return (fading * jnp.cos(phase), fading * jnp.sin(phase))

    back_re, back_im = powers(block_len - 1.0 - offsets)
    ahead_re, ahead_im = powers(offsets + 1.0)
    out_re, out_im = cmul(coef_re[None], coef_im[None], ahead_re, ahead_im)
    lag_re, lag_im = powers(offsets)
    filt = jnp.sum(coef_re[None] * lag_re - coef_im[None] * lag_im, axis=1)
    places = jnp.arange(block_len)
    differ = places[:, None] - places[None, :]
    picked = jnp.take(filt, jnp.maximum(differ, 0), axis=0)
    toeplitz = jnp.where((differ >= 0)[:, :, None], picked, jnp.zeros_like(picked))
    jump_re, jump_im = powers(jnp.full((1,), block_len).astype(jnp.float32))
    return (back_re, back_im, out_re, out_im, toeplitz, jump_re[0], jump_im[0])


def chain(earlier, later):
    sum_re, sum_im = cmul(earlier[0], earlier[1], later[2], later[3])
    pow_re, pow_im = cmul(earlier[2], earlier[3], later[2], later[3])
    return (sum_re + later[0], sum_im + later[1], pow_re, pow_im)


def on_device(
    gate_input, key_input, value_input, decay_rate, frequency, residue, skip_gain, out_weight
):
    highest = lax.Precision.HIGHEST
    signal = key_input.astype(jnp.float32) * value_input.astype(jnp.float32)
    tok_len, chans = signal.shape
    block_len = 16
    block_count = tok_len // block_len
    back_re, back_im, out_re, out_im, toeplitz, jump_re, jump_im = filter_tables(
        decay_rate, frequency, residue, block_len
    )
    blocks = signal.reshape(block_count, block_len, chans)
    entry_re = jnp.einsum("snc,bsc->bnc", back_re, blocks, precision=highest)
    entry_im = jnp.einsum("snc,bsc->bnc", back_im, blocks, precision=highest)

    def advance(state, entry):
        moved_re, moved_im = cmul(jump_re, jump_im, state[0], state[1])
        grown_re, grown_im = cmul(state[2], state[3], jump_re, jump_im)
        return ((moved_re + entry[0], moved_im + entry[1], grown_re, grown_im), state)

    zeros = jnp.zeros(jump_re.shape, jnp.float32)
    ones = jnp.ones(jump_re.shape, jnp.float32)
    final, starts = lax.scan(advance, (zeros, zeros, ones, zeros), (entry_re, entry_im))
    local_re, local_im, device_re, device_im = final
    prefix = entering(
        (local_re, local_im, device_re, device_im), "ctx", chain, (zeros, zeros, ones, zeros)
    )
    incoming_re, incoming_im = (prefix[0], prefix[1])
    carried_re, carried_im = cmul(starts[2], starts[3], incoming_re[None], incoming_im[None])
    begin_re = starts[0] + carried_re
    begin_im = starts[1] + carried_im
    far = jnp.einsum("tnc,bnc->btc", out_re, begin_re, precision=highest) - jnp.einsum(
        "tnc,bnc->btc", out_im, begin_im, precision=highest
    )
    near = jnp.einsum("tsc,bsc->btc", toeplitz, blocks, precision=highest)
    conv = (near + far).reshape(tok_len, chans)
    gated = (gate_input.astype(jnp.float32) * (conv + skip_gain[None, :] * signal)).astype(
        jnp.bfloat16
    )
    whole = lax.all_gather(gated, "ch", axis=1, tiled=True)
    all_rows = lax.all_gather(out_weight, "ctx", axis=0, tiled=True)
    mixed = jnp.dot(whole, all_rows, preferred_element_type=jnp.float32)
    return mixed.astype(jnp.bfloat16)


def solution(mesh):
    placed = (
        P("ctx", "ch"),
        P("ctx", "ch"),
        P("ctx", "ch"),
        P(None, "ch"),
        P(None, "ch"),
        P(None, None, "ch"),
        P("ch"),
        P("ctx", "ch"),
    )
    return jax.shard_map(
        on_device, mesh=mesh, in_specs=placed, out_specs=P("ctx", "ch"), check_vma=False
    )
```

profile of v0, /device:TPU:8, one launch (start us, length us, event | category | flops | bytes accessed | tf_op | source)
XLA Modules:
  0.0 906.5 jit_solution(10265172625318404622)
XLA Ops:
  6.6 1.1 convert_multiply_fusion
  7.7 3.7 copy.51
  11.5 6.1 multiply_add_fusion.1
  17.6 4.1 copy.54
  21.8 9.9 %convolution_bitcast_fusion.1 = f32[16,16,512]{1,0,2:T(8,128)} fusion(f32[16,16,512]{1,0,2:T(8,128)} %copy.51, f32[16,16,512]{1,0,2:T(8,128)} %copy.54), kind=kOutput, calls=%fused_computation.21 | convolution fusion | flops 25165824 | bytes 1572864 | tf_op jit(solution)/shard_map/snc,bsc->bnc/dot_general | solution.py:69
  31.7 3.5 copy.57
  35.2 3.7 copy.56
  38.9 9.9 %convolution_bitcast_fusion = f32[16,16,512]{1,0,2:T(8,128)} fusion(f32[16,16,512]{1,0,2:T(8,128)} %copy.51, f32[16,16,512]{1,0,2:T(8,128)} %copy.56), kind=kOutput, calls=%fused_computation.20 | convolution fusion | flops 25165824 | bytes 1572864 | tf_op jit(solution)/shard_map/snc,bsc->bnc/dot_general | solution.py:70
  48.8 3.5 copy.58
  52.5 14.0 %while.41 = (s32[]{:T(128)}, f32[16,512]{1,0:T(8,128)S(1)}, f32[16,512]{1,0:T(8,128)S(1)}, f32[16,512]{1,0:T(8,128)S(1)}, f32[16,512]{1,0:T(8,128)S(1)}, /*index...) while((s32[]{:T(128)}, f32[16,512]{1,0:T(8,128)S(1)}, ...), condition=%wide.region_2.3_spmd.clone, body=%wide.region_1.2_spmd.clone.sunk | while | flops 180227 | bytes 655533 | solution.py:79
  69.6 1.8 gather_fusion
  71.4 2.0 select_select_fusion
  73.4 4.5 copy.52
  77.9 3.6 copy.60
  81.5 3.7 copy.62
  85.2 12.3 %fusion.17 = f32[512,16,16]{2,1,0:T(8,128)} fusion(f32[16,16,512]{1,0,2:T(8,128)} %copy.51, f32[16,16,512]{1,0,2:T(8,128)} %copy.52), kind=kOutput, calls=%fused_computation.66 | convolution fusion | flops 25165824 | bytes 1572864 | tf_op jit(solution)/shard_map/tsc,bsc->btc/dot_general | solution.py:91
  97.5 115.2 %all-gather.15.cloned.1.call-done = f32[1024,512]{1,0:T(8,128)} async-done(((f32[16,512]{1,0:T(8,128)}), f32[1024,512]{1,0:T(8,128)}) %all-gather.15.cloned.1.call-update) | async-done | bytes 2097168 | tf_op jit(solution)/shard_map/all_gather | solution.py:9
  212.7 139.9 %all-gather.17.cloned.1.call-done = f32[1024,512]{1,0:T(8,128)} async-done(((f32[16,512]{1,0:T(8,128)}), f32[1024,512]{1,0:T(8,128)}) %all-gather.17.cloned.1.call-update) | async-done | bytes 2097168 | tf_op jit(solution)/shard_map/all_gather | solution.py:9
  352.6 139.9 %all-gather.19.cloned.1.call-done = f32[1024,512]{1,0:T(8,128)} async-done(((f32[16,512]{1,0:T(8,128)}), f32[1024,512]{1,0:T(8,128)}) %all-gather.19.cloned.1.call-update) | async-done | bytes 2097168 | tf_op jit(solution)/shard_map/all_gather | solution.py:9
  492.5 139.8 %all-gather.21.cloned.1.call-done = f32[1024,512]{1,0:T(8,128)} async-done(((f32[16,512]{1,0:T(8,128)}), f32[1024,512]{1,0:T(8,128)}) %all-gather.21.cloned.1.call-update) | async-done | bytes 2097168 | tf_op jit(solution)/shard_map/all_gather | solution.py:9
  632.3 54.2 %while.42 = (s32[]{:T(128)}, f32[16,512]{1,0:T(8,128)S(1)}, f32[16,512]{1,0:T(8,128)S(1)}, s32[]{:T(128)}, f32[64,16,512]{2,1,0:T(8,128)}, /*index=5*/f32[64,16,...) while((s32[]{:T(128)}, f32[16,512]{1,0:T(8,128)S(1)}, ...), condition=%wide.region_4.5_spmd.clone, body=%wide.region_3.4_spmd.clone.sunk | while | flops 98308 | bytes 262277 | solution.py:18
  643.5 0.9 fusion.32
  644.3 0.8 fusion.32
  645.2 0.8 fusion.32
  646.1 0.8 fusion.32
  646.9 0.8 fusion.32
  647.8 0.8 fusion.32
  648.6 0.8 fusion.32
  649.5 0.8 fusion.32
  650.4 0.8 fusion.32
  651.2 0.8 fusion.32
  652.1 0.8 fusion.32
  652.9 0.8 fusion.32
  653.8 0.8 fusion.32
  654.7 0.8 fusion.32
  655.5 0.8 fusion.32
  656.4 0.8 fusion.32
  657.2 0.8 fusion.32
  658.1 0.8 fusion.32
  659.0 0.8 fusion.32
  659.8 0.8 fusion.32
  660.7 0.8 fusion.32
  661.5 0.8 fusion.32
  662.4 0.8 fusion.32
  663.3 0.8 fusion.32
  664.1 0.8 fusion.32
  665.0 0.8 fusion.32
  665.8 0.8 fusion.32
  666.7 0.8 fusion.32
  667.6 0.8 fusion.32
  668.4 0.8 fusion.32
  669.3 0.8 fusion.32
  670.1 0.8 fusion.32
  671.0 0.8 fusion.32
  671.9 0.8 fusion.32
  686.8 3.7 copy.59
  690.4 3.6 copy.61
  694.1 9.5 %fusion.18 = f32[512,16,16]{2,1,0:T(8,128)S(1)} fusion(f32[16,16,512]{1,0,2:T(8,128)} %copy.59, f32[16,16,512]{1,0,2:T(8,128)} %copy.60), kind=kOutput, calls=%fused_computation.67 | convolution fusion | flops 25165824 | bytes 1572864 | tf_op jit(solution)/shard_map/tnc,bnc->btc/dot_general | solution.py:88
  703.6 8.5 add_bitcast_fusion
  712.1 2.9 copy.63
  715.0 0.8 fusion.15
  716.5 27.5 %all-gather.11.cloned.1.call-done = bf16[256,4096]{1,0:T(8,128)(2,1)} async-done(((bf16[256,512]{1,0:T(8,128)(2,1)}), bf16[256,4096]{1,0:T(8,128)(2,1)}) %all-gather.11.cloned.1.call-update) | async-done | bytes 2097168 | tf_op jit(solution)/shard_map/all_gather | solution.py:96
  744.0 150.7 %all-gather.13.cloned.1.call-done = bf16[4096,512]{1,0:T(8,128)(2,1)} async-done(((bf16[64,512]{1,0:T(8,128)(2,1)}), bf16[4096,512]{1,0:T(8,128)(2,1)}) %all-gather.13.cloned.1.call-update) | async-done | bytes 4194320 | tf_op jit(solution)/shard_map/all_gather | solution.py:97
  894.6 4.8 convolution_convert_fusion
  (135 shorter events, 41.9 us)
Async XLA Ops:
  6.5 4.8 copy-start.11
  6.5 4.8 copy-start.12
  6.5 4.8 copy-start.10
  6.5 206.1 %all-gather.15.cloned.1.call-start = ((), (), s32[]{:S(2)}) async-start(), calls=%async_computation.2 | async-start | bytes 2129920 | tf_op jit(solution)/shard_map/all_gather | solution.py:9
  66.5 0.6 copy-start.5
  66.6 0.7 copy-start.6
  66.6 1.4 copy-start.3
  66.6 2.1 copy-start.4
  67.2 285.4 %all-gather.17.cloned.1.call-start = ((), (), s32[]{:S(2)}) async-start(), calls=%async_computation.3 | async-start | bytes 2129920 | tf_op jit(solution)/shard_map/all_gather | solution.py:9
  67.9 424.6 %all-gather.19.cloned.1.call-start = ((), (), s32[]{:S(2)}) async-start(), calls=%async_computation.4 | async-start | bytes 2129920 | tf_op jit(solution)/shard_map/all_gather | solution.py:9
  68.7 563.6 %all-gather.21.cloned.1.call-start = ((), (), s32[]{:S(2)}) async-start(), calls=%async_computation.5 | async-start | bytes 2129920 | tf_op jit(solution)/shard_map/all_gather | solution.py:9
  69.2 674.7 %all-gather.11.cloned.1.call-start = ((), (), s32[]{:S(2)}) async-start(), calls=%async_computation | async-start | bytes 2359296 | tf_op jit(solution)/shard_map/all_gather | solution.py:96
  694.1 9.5 %copy-start = (f32[512,16,16]{2,1,0:T(8,128)S(1)}, f32[512,16,16]{2,1,0:T(8,128)}, u32[]{:S(2)}) copy-start(f32[512,16,16]{2,1,0:T(8,128)} %fusion.17) | copy-start | bytes 1572868
  694.1 9.5 %copy-start.1 = (f32[16,16,512]{1,0,2:T(8,128)S(1)}, f32[16,16,512]{1,0,2:T(8,128)}, u32[]{:S(2)}) copy-start(f32[16,16,512]{1,0,2:T(8,128)} %copy.62) | copy-start | bytes 1572868
  694.1 9.5 %copy-start.2 = (f32[16,16,512]{1,0,2:T(8,128)S(1)}, f32[16,16,512]{1,0,2:T(8,128)}, u32[]{:S(2)}) copy-start(f32[16,16,512]{1,0,2:T(8,128)} %copy.61) | copy-start | bytes 1572868
  712.1 2.9 copy-start.7
  712.1 2.9 copy-start.8
  712.1 2.9 copy-start.9
  712.1 2.9 copy-start.13
  715.9 178.7 %all-gather.13.cloned.1.call-start = ((), (), s32[]{:S(2)}) async-start(), calls=%async_computation.1 | async-start | bytes 4259840 | tf_op jit(solution)/shard_map/all_gather | solution.py:97
Sparse Core Ops, SparseCore 0:
  67.3 145.3 all-gather.14
  215.6 136.9 all-gather.16
  355.5 136.9 all-gather.18
  495.3 136.9 all-gather.20
  716.0 27.8 all-gather.10
  746.8 147.8 all-gather.12
where the time goes:
time: 918 us; the launch traced here: 906 us
  waiting for transfers between devices  715 us (78%)
  other arithmetic  76.7 us (8%)
  matrix products  54.8 us (6%)
  local copies, waits for them, and re-layouts  43.3 us (5%)
  between operations  14 us (2%)
    all_gather x4, waiting for transfers between devices, entering(): pieces = jax.tree.map(lambda part: lax.all_gather(part, axis), value)  535 us
    all_gather x1, waiting for transfers between devices, on_device(): all_rows = lax.all_gather(out_weight, 'ctx', axis=0, tiled=True)  151 us
    select_n x63, other arithmetic, hop(): jnp.where(position < mine, new, old)  52.8 us
    all_gather x1, waiting for transfers between devices, on_device(): whole = lax.all_gather(gated, 'ch', axis=1, tiled=True)  27.5 us
    add x17, other arithmetic, cmul(): return (a_re * b_re - a_im * b_im, a_re * b_im + a_im * b_re)  19.1 us
  transfers between devices with their start and end apart: 6, of which 6 were waited for; matrix products, arithmetic and copies ran while one was open for 3% of the time, Pallas kernels for 0%

commit v1 on v0

--- a/solution.py
+++ b/solution.py
@@ -2,6 +2,28 @@
 import jax.numpy as jnp
 from jax import lax
 from jax.sharding import PartitionSpec as P
+
+
+def joined_along(tiles, dim):
+    shape = list(tiles.shape[1:])
+    shape[dim] *= tiles.shape[0]
+    return jnp.moveaxis(tiles, 0, dim).reshape(shape)
+
+
+def ring_gather(x, axis, dim):
+    devices = lax.axis_size(axis)
+    pairs = [(i, (i + 1) % devices) for i in range(devices)]
+    back = [(b, a) for a, b in pairs]
+    lower, upper = ([], [])
+    for turn in range(devices - 1):
+        if turn % 2 == 0:
+            lower.append(lax.ppermute(lower[-1] if lower else x, axis, pairs))
+        else:
+            upper.append(lax.ppermute(upper[-1] if upper else x, axis, back))
+    blocks = jnp.stack([*lower[::-1], x, *upper])
+    shift = lax.axis_index(axis) - len(lower)
+    blocks = blocks[(jnp.arange(devices) - shift) % devices]
+    return joined_along(blocks, dim)
 
 
 def entering(value, axis, join, neutral):
@@ -93,7 +115,7 @@
     gated = (gate_input.astype(jnp.float32) * (conv + skip_gain[None, :] * signal)).astype(
         jnp.bfloat16
     )
-    whole = lax.all_gather(gated, "ch", axis=1, tiled=True)
+    whole = ring_gather(gated, "ch", 1)
     all_rows = lax.all_gather(out_weight, "ctx", axis=0, tiled=True)
     mixed = jnp.dot(whole, all_rows, preferred_element_type=jnp.float32)
     return mixed.astype(jnp.bfloat16)

time: 918 us -> 801 us (0.87)
  waiting for transfers between devices: 715 us -> 582 us
  local copies, waits for them, and re-layouts: 43.3 us -> 53.8 us
    all_gather x1, waiting for transfers between devices: 151 us -> 28.2 us  [on_device(): all_rows = lax.all_gather(out_weight, 'ctx', axis=0, tiled=True)]
    all_gather x1 -> x0, waiting for transfers between devices: 27.5 us -> none  [on_device(): whole = lax.all_gather(gated, 'ch', axis=1, tiled=True)]
    ppermute x0 -> x7, waiting for transfers between devices: none -> 17 us  [the longest x4 16.7 us: ring_gather(): lower.append(lax.ppermute(lower[-1] if lower else x, axis, pairs))]
  transfers between devices with their start and end apart: 6 -> 12, of which waited for: 6 -> 10; matrix products, arithmetic and copies ran while one was open for 3% -> 15% of each run, Pallas kernels for 0% -> 0%
where the time goes in v1:
time: 801 us; the launch traced here: 789 us
  waiting for transfers between devices  582 us (73%)
  other arithmetic  76.1 us (10%)
  matrix products  54.8 us (7%)
  local copies, waits for them, and re-layouts  53.8 us (7%)
  between operations  13.7 us (2%)
    all_gather x4, waiting for transfers between devices, entering(): pieces = jax.tree.map(lambda part: lax.all_gather(part, axis), value)  534 us
    select_n x63, other arithmetic, hop(): jnp.where(position < mine, new, old)  52.8 us
    all_gather x1, waiting for transfers between devices, on_device(): all_rows = lax.all_gather(out_weight, 'ctx', axis=0, tiled=True)  28.2 us
    add x17, other arithmetic, cmul(): return (a_re * b_re - a_im * b_im, a_re * b_im + a_im * b_re)  19.1 us
    ppermute x4, waiting for transfers between devices, ring_gather(): lower.append(lax.ppermute(lower[-1] if lower else x, axis, pairs))  16.7 us
  transfers between devices with their start and end apart: 12, of which 10 were waited for; matrix products, arithmetic and copies ran while one was open for 15% of the time, Pallas kernels for 0%

profile of v1, /device:TPU:8, one launch (start us, length us, event | category | flops | bytes accessed | tf_op | source)
XLA Modules:
  0.0 788.7 jit_solution(7902737293759218759)
XLA Ops:
  6.6 1.1 convert_multiply_fusion
  7.7 3.7 copy.53
  11.6 6.1 multiply_add_fusion.1
  17.7 4.1 copy.56
  21.8 9.9 %convolution_bitcast_fusion.1 = f32[16,16,512]{1,0,2:T(8,128)} fusion(f32[16,16,512]{1,0,2:T(8,128)} %copy.53, f32[16,16,512]{1,0,2:T(8,128)} %copy.56), kind=kOutput, calls=%fused_computation.22 | convolution fusion | flops 25165824 | bytes 1572864 | tf_op jit(solution)/shard_map/snc,bsc->bnc/dot_general | solution.py:91
  31.7 3.5 copy.59
  35.2 3.7 copy.58
  38.9 9.8 %convolution_bitcast_fusion = f32[16,16,512]{1,0,2:T(8,128)} fusion(f32[16,16,512]{1,0,2:T(8,128)} %copy.53, f32[16,16,512]{1,0,2:T(8,128)} %copy.58), kind=kOutput, calls=%fused_computation.21 | convolution fusion | flops 25165824 | bytes 1572864 | tf_op jit(solution)/shard_map/snc,bsc->bnc/dot_general | solution.py:92
  48.7 3.5 copy.60
  52.5 14.0 %while.41 = (s32[]{:T(128)}, f32[16,512]{1,0:T(8,128)S(1)}, f32[16,512]{1,0:T(8,128)S(1)}, f32[16,512]{1,0:T(8,128)S(1)}, f32[16,512]{1,0:T(8,128)S(1)}, /*index...) while((s32[]{:T(128)}, f32[16,512]{1,0:T(8,128)S(1)}, ...), condition=%wide.region_2.3_spmd.clone, body=%wide.region_1.2_spmd.clone.sunk | while | flops 180227 | bytes 655533 | solution.py:101
  69.9 1.8 gather_fusion
  71.7 2.0 select_select_fusion
  73.7 4.5 copy.54
  78.2 12.3 %fusion.19 = f32[512,16,16]{2,1,0:T(8,128)} fusion(f32[16,16,512]{1,0,2:T(8,128)} %copy.53, f32[16,16,512]{1,0,2:T(8,128)} %copy.54), kind=kOutput, calls=%fused_computation.82 | convolution fusion | flops 25165824 | bytes 1572864 | tf_op jit(solution)/shard_map/tsc,bsc->btc/dot_general | solution.py:113
  90.5 3.6 copy.62
  94.1 3.7 copy.64
  97.8 114.8 %all-gather.12.cloned.1.call-done = f32[1024,512]{1,0:T(8,128)} async-done(((f32[16,512]{1,0:T(8,128)}), f32[1024,512]{1,0:T(8,128)}) %all-gather.12.cloned.1.call-update) | async-done | bytes 2097168 | tf_op jit(solution)/shard_map/all_gather | solution.py:31
  212.6 139.9 %all-gather.14.cloned.1.call-done = f32[1024,512]{1,0:T(8,128)} async-done(((f32[16,512]{1,0:T(8,128)}), f32[1024,512]{1,0:T(8,128)}) %all-gather.14.cloned.1.call-update) | async-done | bytes 2097168 | tf_op jit(solution)/shard_map/all_gather | solution.py:31
  352.5 139.9 %all-gather.16.cloned.1.call-done = f32[1024,512]{1,0:T(8,128)} async-done(((f32[16,512]{1,0:T(8,128)}), f32[1024,512]{1,0:T(8,128)}) %all-gather.16.cloned.1.call-update) | async-done | bytes 2097168 | tf_op jit(solution)/shard_map/all_gather | solution.py:31
  492.5 139.8 %all-gather.18.cloned.1.call-done = f32[1024,512]{1,0:T(8,128)} async-done(((f32[16,512]{1,0:T(8,128)}), f32[1024,512]{1,0:T(8,128)}) %all-gather.18.cloned.1.call-update) | async-done | bytes 2097168 | tf_op jit(solution)/shard_map/all_gather | solution.py:31
  632.2 54.2 %while.42 = (s32[]{:T(128)}, f32[16,512]{1,0:T(8,128)S(1)}, f32[16,512]{1,0:T(8,128)S(1)}, s32[]{:T(128)}, f32[64,16,512]{2,1,0:T(8,128)}, /*index=5*/f32[64,16,...) while((s32[]{:T(128)}, f32[16,512]{1,0:T(8,128)S(1)}, ...), condition=%wide.region_4.5_spmd.clone, body=%wide.region_3.4_spmd.clone.sunk | while | flops 98308 | bytes 262277 | solution.py:40
  633.1 0.8 fusion.34
  633.9 0.8 fusion.34
  634.8 0.8 fusion.34
  635.7 0.8 fusion.34
  636.5 0.8 fusion.34
  637.4 0.8 fusion.34
  638.2 0.8 fusion.34
  639.1 0.8 fusion.34
  640.0 0.8 fusion.34
  640.8 0.8 fusion.34
  641.7 0.8 fusion.34
  642.5 0.8 fusion.34
  643.4 0.8 fusion.34
  644.3 0.8 fusion.34
  645.1 0.8 fusion.34
  646.0 0.8 fusion.34
  646.8 0.8 fusion.34
  647.7 0.8 fusion.34
  653.7 0.8 fusion.34
  658.0 0.8 fusion.34
  661.5 0.8 fusion.34
  664.9 0.8 fusion.34
  667.5 0.8 fusion.34
  668.4 0.8 fusion.34
  672.7 0.8 fusion.34
  675.2 0.8 fusion.34
  683.0 0.8 fusion.34
  686.7 3.7 copy.61
  690.4 3.6 copy.63
  694.1 9.5 %fusion.20 = f32[512,16,16]{2,1,0:T(8,128)S(1)} fusion(f32[16,16,512]{1,0,2:T(8,128)} %copy.61, f32[16,16,512]{1,0,2:T(8,128)} %copy.62), kind=kOutput, calls=%fused_computation.83 | convolution fusion | flops 25165824 | bytes 1572864 | tf_op jit(solution)/shard_map/tnc,bnc->btc/dot_general | solution.py:110
  703.6 8.6 %add_bitcast_fusion = f32[16,16,512]{1,0,2:T(8,128)} fusion(f32[512,16,16]{2,1,0:T(8,128)S(1)} %copy-done, f32[512,16,16]{2,1,0:T(8,128)S(1)} %fusion.20, f32[16,16,512]{1,0,2:T(8,128)S(1)} %copy-done.2, f32[16,16,512]{1,0,2:T(8,128)S(1)} %copy-done.1), kind=kOutput, calls=%fused_computation.20 | convolution fusion | flops 25427968 | bytes 2621440 | tf_op jit(solution)/shard_map/tnc,bnc->btc/dot_general | solution.py:110
  712.1 2.9 copy.65
  715.2 5.8 collective-permute-done
  721.0 1.7 collective-permute-start.4
  722.8 4.1 collective-permute-done.1
  726.8 2.1 collective-permute-start.5
  729.0 3.7 collective-permute-done.2
  732.9 2.3 collective-permute-start.6
  735.2 3.3 collective-permute-done.3
  744.2 2.3 gather_fusion.1
  746.5 2.4 copy.66
  748.9 28.2 %all-gather.10.cloned.1.call-done = bf16[4096,512]{1,0:T(8,128)(2,1)} async-done(((bf16[64,512]{1,0:T(8,128)(2,1)}), bf16[4096,512]{1,0:T(8,128)(2,1)}) %all-gather.10.cloned.1.call-update) | async-done | bytes 4194320 | tf_op jit(solution)/shard_map/all_gather | solution.py:119
  777.2 4.8 convolution_convert_fusion
  (158 shorter events, 53.8 us)
Async XLA Ops:
  6.5 4.9 copy-start.11
  6.5 4.9 copy-start.12
  6.5 4.9 copy-start.10
  6.5 206.1 %all-gather.12.cloned.1.call-start = ((), (), s32[]{:S(2)}) async-start(), calls=%async_computation.1 | async-start | bytes 2129920 | tf_op jit(solution)/shard_map/all_gather | solution.py:31
  66.5 0.6 copy-start.5
  66.5 0.7 copy-start.6
  66.5 1.4 copy-start.3
  66.5 2.1 copy-start.4
  67.1 285.4 %all-gather.14.cloned.1.call-start = ((), (), s32[]{:S(2)}) async-start(), calls=%async_computation.2 | async-start | bytes 2129920 | tf_op jit(solution)/shard_map/all_gather | solution.py:31
  67.9 424.6 %all-gather.16.cloned.1.call-start = ((), (), s32[]{:S(2)}) async-start(), calls=%async_computation.3 | async-start | bytes 2129920 | tf_op jit(solution)/shard_map/all_gather | solution.py:31
  68.6 563.6 %all-gather.18.cloned.1.call-start = ((), (), s32[]{:S(2)}) async-start(), calls=%async_computation.4 | async-start | bytes 2129920 | tf_op jit(solution)/shard_map/all_gather | solution.py:31
  69.2 708.0 %all-gather.10.cloned.1.call-start = ((), (), s32[]{:S(2)}) async-start(), calls=%async_computation | async-start | bytes 4259840 | tf_op jit(solution)/shard_map/all_gather | solution.py:119
  694.1 9.5 %copy-start = (f32[512,16,16]{2,1,0:T(8,128)S(1)}, f32[512,16,16]{2,1,0:T(8,128)}, u32[]{:S(2)}) copy-start(f32[512,16,16]{2,1,0:T(8,128)} %fusion.19) | copy-start | bytes 1572868
  694.1 9.5 %copy-start.1 = (f32[16,16,512]{1,0,2:T(8,128)S(1)}, f32[16,16,512]{1,0,2:T(8,128)}, u32[]{:S(2)}) copy-start(f32[16,16,512]{1,0,2:T(8,128)} %copy.64) | copy-start | bytes 1572868
  694.1 9.5 %copy-start.2 = (f32[16,16,512]{1,0,2:T(8,128)S(1)}, f32[16,16,512]{1,0,2:T(8,128)}, u32[]{:S(2)}) copy-start(f32[16,16,512]{1,0,2:T(8,128)} %copy.63) | copy-start | bytes 1572868
  712.1 2.9 copy-start.7
  712.1 2.9 copy-start.8
  712.1 2.9 copy-start.9
  712.1 2.9 copy-start.13
  715.2 5.8 collective-permute-start
  721.0 5.8 collective-permute-start.1
  721.0 5.8 collective-permute-start.4
  726.8 5.8 collective-permute-start.2
  726.8 6.0 collective-permute-start.5
  732.6 5.8 collective-permute-start.3
  732.9 10.7 %collective-permute-start.6 = (bf16[256,512]{1,0:T(8,128)(2,1)S(1)}, bf16[256,512]{1,0:T(8,128)(2,1)S(1)}, u32[]{:S(2)}, u32[]{:S(2)}) collective-permute-start(bf16[256,512]{1,0:T(8,128)(2,1)S(1)} %collective-permute-done.5), channel_id=1, source_target_pairs={{1,0},{2,1},{3,2},{4,3},{5,4},{6,5},{7,6},{0,7},{9,8},{10,9},{11,1... | collective-permute-start | bytes 786440 | tf_op jit(solution)/shard_map/ppermute | solution.py:22
Sparse Core Ops, SparseCore 0:
  67.2 145.3 all-gather.11
  215.5 136.9 all-gather.13
  355.5 136.9 all-gather.15
  495.3 136.9 all-gather.17
  635.0 142.0 all-gather.9
